TPU v7x, 256 devices: a whole 4x4x8 slice. The times are simulated.
256 devices in a mesh: batch: 16 (over x, y_hi, core), space: 16 (over z, y_lo).
Axes of the slice: x: 4, y: 4 (y_hi: 2, y_lo: 2; y = y_hi * 2 + y_lo), z: 8, core: 2. Of those that a mesh axis runs over, the one named last changes fastest.
Arguments:
- snapshots: bfloat16 [16, 64, 32, 1024], P('batch', None, 'space'), may hold values from -6 to 6
- cotangent: bfloat16 [16, 64, 32, 1024], P('batch', None, 'space'), may hold values from -6 to 6
- mode_weight: bfloat16 [16, 16, 24, 64, 64], P('batch', 'space'), may hold values from -0.75 to 0.75
- conv_weight: bfloat16 [3, 3, 3, 64, 64], replicated, may hold values from -0.15625 to 0.15625
Outputs:
- activated: bfloat16 [16, 64, 32, 1024], P('batch', None, 'space')
- input_gradient: bfloat16 [16, 64, 32, 1024], P('batch', None, 'space')
- mode_gradient: float32 [16, 16, 24, 64, 64], P('batch', 'space')
- conv_gradient: float32 [3, 3, 3, 64, 64], replicated
All inputs are finite; a program needn't handle non-finite values.
Results may differ from a plain program's by a relative error of at most 0.02.
Values may be sent and summed in bfloat16 or wider, within the bound.
A program may use at most 128 MiB of HBM per device.

v0:
```python
import math
import jax
import jax.numpy as jnp
from jax import lax
from jax.sharding import PartitionSpec as P

KX = 8
KY = 8
KZ = 12
NX = 32
NY = 32
inv_root_two = 1.0 / math.sqrt(2.0)
inv_root_two_pi = 1.0 / math.sqrt(2.0 * math.pi)


def extended_2(cells, sides, width):
    for axis, dim in sides:
        count = lax.axis_size(axis)
        ends = count - 1
        head = lax.slice_in_dim(cells, 0, width, axis=dim)
        tail = lax.slice_in_dim(cells, cells.shape[dim] - width, cells.shape[dim], axis=dim)
        cells = jnp.concatenate(
            [
                lax.ppermute(tail, axis, [(i, (i + 1) % count) for i in range(ends)]),
                cells,
                lax.ppermute(head, axis, [((i + 1) % count, i) for i in range(ends)]),
            ],
            axis=dim,
        )
    return cells


def basis_rows(half_count, length):
    row_index = lax.broadcasted_iota(jnp.int32, (2 * half_count, length), 0)
    cell_index = lax.broadcasted_iota(jnp.int32, (2 * half_count, length), 1)
    frequency = jnp.where(row_index < half_count, row_index, row_index - half_count + 1)
    phases = (frequency * cell_index % length).astype(jnp.float32) * (2.0 * math.pi / length)
    return jnp.where(row_index < half_count, jnp.cos(phases), jnp.sin(phases))


def make_tables(count_x, count_y, count_z, length_x, length_y, length_z):
    across = basis_rows(count_x, length_x)
    along_y = basis_rows(count_y, length_y)
    depth_rows = basis_rows(count_z, length_z)
    modes_x = 2 * count_x
    modes_y = 2 * count_y
    outer_table = (across[:, None, :, None] * along_y[None, :, None, :]).reshape(
        modes_x * modes_y, length_x * length_y
    )
    plane_analysis = (outer_table * (2.0 / math.sqrt(length_x * length_y))).astype(jnp.bfloat16)
    plane_synthesis = (outer_table.T * (2.0 / math.sqrt(modes_x * modes_y))).astype(jnp.bfloat16)
    depth_analysis = (depth_rows * math.sqrt(2.0 / length_z)).astype(jnp.bfloat16)
    depth_synthesis = (depth_rows.T * math.sqrt(2.0 / (2 * count_z))).astype(jnp.bfloat16)
    return (plane_analysis, plane_synthesis, depth_analysis, depth_synthesis)


def rim(values):
    return extended_2(values, (("space", 1),), 1)


def widen(values):
    channels, depth_cells, plane = values.shape
    extended = rim(values)
    return jnp.pad(
        extended.reshape(channels, depth_cells + 2, NX, NY), ((0, 0), (0, 0), (1, 1), (1, 1))
    )


def to_pencils(values):
    return lax.all_to_all(values, "space", split_axis=3, concat_axis=1, tiled=True)


def to_slabs(values):
    return lax.all_to_all(values, "space", split_axis=1, concat_axis=3, tiled=True)


def stacked_window(padded, offset_x, offset_y):
    channels = padded.shape[0]
    depth_cells = padded.shape[1] - 2
    window = padded[:, :, offset_x : offset_x + NX, offset_y : offset_y + NY]
    stacked = jnp.stack([window[:, offset_z : offset_z + depth_cells] for offset_z in range(3)], 0)
    return stacked.reshape(3, channels, depth_cells * NX * NY)


def stencil(padded, kernel):
    depth_cells = padded.shape[1] - 2
    summed = jnp.zeros((kernel.shape[4], depth_cells * NX * NY), jnp.float32)
    for offset_x in range(3):
        for offset_y in range(3):
            stacked = stacked_window(padded, offset_x, offset_y)
            summed = summed + lax.dot_general(
                kernel[:, offset_x, offset_y],
                stacked,
                (((0, 1), (0, 1)), ((), ())),
                preferred_element_type=jnp.float32,
            )
    return summed


def kernel_terms(padded, pre_flat):
    pieces = []
    for offset_x in range(3):
        row_pieces = []
        for offset_y in range(3):
            stacked = stacked_window(padded, offset_x, offset_y)
            row_pieces.append(
                lax.dot_general(
                    stacked, pre_flat, (((2,), (1,)), ((), ())), preferred_element_type=jnp.float32
                )
            )
        pieces.append(jnp.stack(row_pieces, 1))
    return jnp.stack(pieces, 1)


def shards(snapshots, cotangent, mode_weight, conv_weight):
    local_field = snapshots[0]
    channels, depth_cells, plane = local_field.shape
    total_depth = depth_cells * lax.axis_size("space")
    modes_x = 2 * KX
    modes_y = 2 * KY
    plane_analysis, plane_synthesis, depth_analysis, depth_synthesis = make_tables(
        KX, KY, KZ, NX, NY, total_depth
    )
    padded = widen(local_field)
    plane_coef = lax.dot_general(
        local_field.reshape(channels * depth_cells, plane),
        plane_analysis,
        (((1,), (1,)), ((), ())),
        preferred_element_type=jnp.float32,
    )
    plane_coef = plane_coef.astype(jnp.bfloat16).reshape(channels, depth_cells, modes_x, modes_y)
    coef = jnp.einsum(
        "czxy,pz->cpxy", to_pencils(plane_coef), depth_analysis, preferred_element_type=jnp.float32
    ).astype(jnp.bfloat16)
    full_weight = lax.all_gather(mode_weight, "batch", axis=0, tiled=True)
    mixed = jnp.einsum(
        "ipxy,xypio->opxy", coef, full_weight, preferred_element_type=jnp.float32
    ).astype(jnp.bfloat16)
    depth_back = jnp.einsum(
        "opxy,zp->ozxy", mixed, depth_synthesis, preferred_element_type=jnp.float32
    ).astype(jnp.bfloat16)
    slab_back = to_slabs(depth_back)
    spectral = lax.dot_general(
        slab_back.reshape(channels * depth_cells, modes_x * modes_y),
        plane_synthesis,
        (((1,), (1,)), ((), ())),
        preferred_element_type=jnp.float32,
    )
    pre = spectral.reshape(channels, depth_cells * plane) + stencil(padded, conv_weight)
    normal_cdf = 0.5 * (1.0 + lax.erf(pre * inv_root_two))
    density = jnp.exp(-0.5 * pre * pre) * inv_root_two_pi
    activated = (pre * normal_cdf).astype(jnp.bfloat16).reshape(channels, depth_cells, plane)
    pre_grad = (
        cotangent[0].reshape(channels, depth_cells * plane).astype(jnp.float32)
        * (normal_cdf + pre * density)
    ).astype(jnp.bfloat16)
    back_plane = jnp.dot(
        pre_grad.reshape(channels * depth_cells, plane),
        plane_synthesis,
        preferred_element_type=jnp.float32,
    )
    back_plane = back_plane.astype(jnp.bfloat16).reshape(channels, depth_cells, modes_x, modes_y)
    mixed_grad = jnp.einsum(
        "ozxy,zp->opxy", to_pencils(back_plane), depth_synthesis, preferred_element_type=jnp.float32
    ).astype(jnp.bfloat16)
    coef_grad = jnp.einsum(
        "opxy,xypio->ipxy", mixed_grad, full_weight, preferred_element_type=jnp.float32
    ).astype(jnp.bfloat16)
    mode_gradient = lax.psum_scatter(
        jnp.einsum("ipxy,opxy->xypio", coef, mixed_grad, preferred_element_type=jnp.float32).astype(
            jnp.bfloat16
        ),
        "batch",
        scatter_dimension=0,
        tiled=True,
    ).astype(jnp.float32)
    depth_grad = jnp.einsum(
        "ipxy,pz->izxy", coef_grad, depth_analysis, preferred_element_type=jnp.float32
    ).astype(jnp.bfloat16)
    slab_grad = to_slabs(depth_grad)
    spectral_grad = jnp.dot(
        slab_grad.reshape(channels * depth_cells, modes_x * modes_y),
        plane_analysis,
        preferred_element_type=jnp.float32,
    )
    flipped = jnp.transpose(conv_weight[::-1, ::-1, ::-1], (0, 1, 2, 4, 3))
    local_grad = stencil(widen(pre_grad.reshape(channels, depth_cells, plane)), flipped)
    input_gradient = (
        (spectral_grad.reshape(channels, depth_cells * plane) + local_grad)
        .astype(jnp.bfloat16)
        .reshape(channels, depth_cells, plane)
    )
    kernel_local = kernel_terms(padded, pre_grad)
    kernel_total = lax.psum(kernel_local, ("batch", "space"))
    conv_gradient = kernel_total / math.sqrt(lax.axis_size("batch") * total_depth * plane)
    return (activated[None], input_gradient[None], mode_gradient, conv_gradient)


def solution(mesh):
    in_specs = (
        P("batch", None, "space", None),
        P("batch", None, "space", None),
        P("batch", "space", None, None, None),
        P(),
    )
    out_specs = (
        P("batch", None, "space", None),
        P("batch", None, "space", None),
        P("batch", "space", None, None, None),
        P(),
    )
    return jax.shard_map(shards, mesh=mesh, in_specs=in_specs, out_specs=out_specs, check_vma=False)
```

profile of v0, /device:TPU:2, one launch (start us, length us, event | category | flops | bytes accessed | tf_op | source)
XLA Modules:
  0.0 513.8 jit_solution(1458009510099474854)
XLA Ops:
  10.0 4.2 collective-permute-start
  15.5 1.8 reshape_squeeze.4
  17.4 2.2 fusion.6
  19.5 3.6 convert_element_type.165
  25.6 1.8 copy.99
  28.2 11.5 %all-to-all-start = ((bf16[16,2,1024]{2,1,0:T(2,128)(2,1)}), bf16[16,2,1024]{2,1,0:T(2,128)(2,1)S(1)}, u32[]{:S(2)}, u32[]{:S(2)}) async-start(bf16[16,2,1024]{2,1,0:T(2,128)(2,1)} %reshape.401), calls=%async_computation | async-start | bytes 131072 | tf_op jit(solution)/shard_map/all_to_all | solution.py:70
  40.6 1.8 copy.190
  42.4 2.9 convert_element_type.178
  45.3 3.4 all-to-all-done
  53.0 1.6 select_maximum_fusion.2
  54.6 1.5 fusion.196
  56.1 1.9 copy.109
  58.0 1.9 copy.107
  61.8 3.9 fusion.195
  65.7 2.0 copy.134
  67.7 2.0 copy.133
  69.7 1.9 copy.132
  71.6 1.9 copy.130
  73.6 1.9 copy.129
  75.5 1.9 copy.128
  77.5 1.9 copy.126
  81.2 2.0 copy.119
  83.2 2.0 copy.118
  85.2 1.9 copy.117
  87.1 1.9 copy.115
  89.0 1.9 copy.114
  93.7 1.4 convolution_bitcast_fusion.17
  95.2 1.5 fusion.19
  99.4 4.6 fusion.3
  105.2 5.1 %all-to-all-start.1 = ((bf16[16,2,1024]{2,1,0:T(2,128)(2,1)}), bf16[16,2,1024]{2,1,0:T(2,128)(2,1)}, u32[]{:S(2)}, u32[]{:S(2)}) async-start(bf16[16,2,1024]{2,1,0:T(2,128)(2,1)} %reshape.403), calls=%async_computation.1 | async-start | bytes 131072 | tf_op jit(solution)/shard_map/all_to_all | solution.py:74
  110.3 2.4 fusion.13
  115.5 3.9 all-to-all-done.1
  122.1 2.6 fusion.85
  124.7 2.1 convolution_bitcast_fusion.25
  136.7 4.3 all-to-all-start.2
  142.4 7.8 %all-to-all-done.2 = bf16[16,2,1024]{2,1,0:T(2,128)(2,1)S(1)} async-done(((bf16[16,2,1024]{2,1,0:T(2,128)(2,1)}), bf16[16,2,1024]{2,1,0:T(2,128)(2,1)S(1)}, u32[]{:S(2)}, u32[]{:S(2)}) %all-to-all-start.2) | async-done | bytes 65568 | tf_op jit(solution)/shard_map/all_to_all | solution.py:70
  150.7 5.8 %fusion = bf16[16,1,24,64,64]{4,3,2,1,0:T(8,128)(2,1)} fusion(f32[16,24,64]{2,1,0:T(8,128)S(1)} %get-tuple-element.76, f32[16,24,64]{2,1,0:T(8,128)S(1)} %get-tuple-element.77), kind=kLoop, calls=%fused_computation.1 | loop fusion | flops 3145728 | bytes 3342336 | tf_op jit(solution)/shard_map/convert_element_type | solution.py:170
  159.6 2.6 collective-permute-start.2
  162.2 1.3 collective-permute-start.3
  163.5 6.1 %fusion.1 = bf16[24,16,1,64]{3,2,1,0:T(2,128)(2,1)S(1)} fusion(bf16[64,24,16,1]{0,1,2,3:T(8,128)(2,1)S(1)} %bitcast.459, bf16[16,1,24,64,64]{4,3,2,1,0:T(8,128)(2,1)} %all-gather.2.cloned.1.call-done), kind=kOutput, calls=%fused_computation.4 | convolution fusion | flops 3145728 | bytes 3244032 | tf_op jit(solution)/shard_map/opxy,xypio->ipxy/dot_general | solution.py:166
  170.8 6.4 %all-to-all-start.3 = ((bf16[16,2,1024]{2,1,0:T(2,128)(2,1)}), bf16[16,2,1024]{2,1,0:T(2,128)(2,1)S(1)}, u32[]{:S(2)}, u32[]{:S(2)}) async-start(bf16[16,2,1024]{2,1,0:T(2,128)(2,1)} %reshape.407), calls=%async_computation.3 | async-start | bytes 131072 | tf_op jit(solution)/shard_map/all_to_all | solution.py:74
  179.3 1.6 select_maximum_fusion
  180.8 1.5 fusion.194
  182.3 2.0 copy.148
  184.3 1.9 copy.152
  188.9 3.8 fusion.193
  192.8 1.3 copy.147
  194.1 2.0 copy.172
  196.1 1.9 copy.171
  198.0 1.9 copy.170
  200.0 1.9 copy.169
  201.9 1.9 copy.168
  203.8 1.9 copy.167
  207.6 2.0 copy.164
  209.6 1.9 copy.163
  211.6 2.0 copy.162
  213.5 2.0 copy.159
  215.5 1.9 copy.158
  222.0 1.4 convolution_bitcast_fusion.4
  224.6 2.3 convolution_bitcast_fusion.1
  232.5 172.3 %all-reduce.4.cloned.1.call-done = f32[3,3,3,64,64]{4,3,0,2,1:T(8,128)} async-done(((f32[3,3,3,64,64]{4,3,0,2,1:T(8,128)}), f32[3,3,3,64,64]{4,3,0,2,1:T(8,128)}) %all-reduce.4.cloned.1.call-update) | async-done | bytes 442384 | tf_op jit(solution)/shard_map/psum | solution.py:194
  409.0 2.4 fusion.30
  412.3 92.8 %reduce-scatter.2.cloned.1.call-done = bf16[1,1,24,64,64]{4,3,2,1,0:T(8,128)(2,1)} async-done(((bf16[16,1,24,64,64]{4,3,2,1,0:T(8,128)(2,1)}), bf16[1,1,24,64,64]{4,3,2,1,0:T(8,128)(2,1)}) %reduce-scatter.2.cloned.1.call-update) | async-done | bytes 196624 | tf_op jit(solution)/shard_map/reduce_scatter | solution.py:169
  505.1 2.0 convert_element_type.196
  (293 shorter events, 66.7 us)
Async XLA Ops:
  7.2 92.2 %all-gather.2.cloned.1.call-start = ((), (), s32[]{:S(2)}) async-start(), calls=%async_computation.5 | async-start | bytes 6684672 | tf_op jit(solution)/shard_map/all_gather | solution.py:135
  10.0 40.0 %collective-permute-start = (bf16[64,1,1024]{0,2,1:T(8,128)(2,1)}, bf16[64,1,1024]{0,2,1:T(8,128)(2,1)}, u32[]{:S(2)}, u32[]{:S(2)}) collective-permute-start(bf16[64,1,1024]{0,2,1:T(8,128)(2,1)} %get-tuple-element.72), channel_id=1, source_target_pairs={{0,1},{1,2},{2,3},{3,4},{4,5},{5,6},{6,7},{7,8},{8,9},{9,10},{10,1... | collective-permute-start | bytes 393224 | tf_op jit(solution)/shard_map/ppermute | solution.py:24
  14.2 35.8 %collective-permute-start.1 = (bf16[64,1,1024]{0,2,1:T(8,128)(2,1)}, bf16[64,1,1024]{0,2,1:T(8,128)(2,1)}, u32[]{:S(2)}, u32[]{:S(2)}) collective-permute-start(bf16[64,1,1024]{0,2,1:T(8,128)(2,1)} %get-tuple-element.73), channel_id=1, source_target_pairs={{1,0},{2,1},{3,2},{4,3},{5,4},{6,5},{7,6},{8,7},{9,8},{10,9},{11,1... | collective-permute-start | bytes 393224 | tf_op jit(solution)/shard_map/ppermute | solution.py:26
  19.5 20.2 %copy-start.1 = (bf16[1,64,2,1024]{3,2,1,0:T(2,128)(2,1)S(1)}, bf16[1,64,2,1024]{3,2,1,0:T(2,128)(2,1)}, u32[]{:S(2)}) copy-start(bf16[1,64,2,1024]{3,2,1,0:T(2,128)(2,1)} %param.4) | copy-start | bytes 786436
  28.2 20.6 %all-to-all-start = ((bf16[16,2,1024]{2,1,0:T(2,128)(2,1)}), bf16[16,2,1024]{2,1,0:T(2,128)(2,1)S(1)}, u32[]{:S(2)}, u32[]{:S(2)}) async-start(bf16[16,2,1024]{2,1,0:T(2,128)(2,1)} %reshape.401), calls=%async_computation | async-start | bytes 131072 | tf_op jit(solution)/shard_map/all_to_all | solution.py:70
  65.7 13.7 %copy-start.9 = (bf16[64,2,32,32]{0,3,2,1:T(8,128)(2,1)S(1)}, bf16[64,2,32,32]{0,3,2,1:T(8,128)(2,1)}, u32[]{:S(2)}) copy-start(bf16[64,2,32,32]{0,3,2,1:T(8,128)(2,1)} %get-tuple-element.49) | copy-start | bytes 786436
  67.7 12.6 %copy-start.7 = (bf16[64,2,32,32]{0,3,2,1:T(8,128)(2,1)S(1)}, bf16[64,2,32,32]{0,3,2,1:T(8,128)(2,1)}, u32[]{:S(2)}) copy-start(bf16[64,2,32,32]{0,3,2,1:T(8,128)(2,1)} %get-tuple-element.50) | copy-start | bytes 786436
  80.3 11.6 %copy-start.5 = (bf16[64,2,32,32]{0,3,2,1:T(8,128)(2,1)S(1)}, bf16[64,2,32,32]{0,3,2,1:T(8,128)(2,1)}, u32[]{:S(2)}) copy-start(bf16[64,2,32,32]{0,3,2,1:T(8,128)(2,1)} %get-tuple-element.57) | copy-start | bytes 786436
  81.2 11.6 %copy-start.3 = (bf16[64,2,32,32]{0,3,2,1:T(8,128)(2,1)S(1)}, bf16[64,2,32,32]{0,3,2,1:T(8,128)(2,1)}, u32[]{:S(2)}) copy-start(bf16[64,2,32,32]{0,3,2,1:T(8,128)(2,1)} %get-tuple-element.58) | copy-start | bytes 786436
  83.2 10.5 %copy-start.22 = (bf16[1,64,2048]{2,1,0:T(8,128)(2,1)S(1)}, bf16[1,64,2048]{2,1,0:T(8,128)(2,1)}, u32[]{:S(2)}) copy-start(bf16[1,64,2048]{2,1,0:T(8,128)(2,1)} %copy.107) | copy-start | bytes 786436
  91.8 3.3 copy-start.19
  92.8 3.9 copy-start.55
  92.8 3.9 copy-start.57
  93.7 3.3 copy-start.49
  93.7 3.3 copy-start.51
  93.7 3.4 copy-start.53
  99.4 10.9 %copy-start.30 = (bf16[1,64,2048]{2,1,0:T(8,128)(2,1)S(1)}, bf16[1,64,2048]{2,1,0:T(8,128)(2,1)}, u32[]{:S(2)}) copy-start(bf16[1,64,2048]{2,1,0:T(8,128)(2,1)} %copy.134) | copy-start | bytes 786436
  99.4 10.9 %copy-start.32 = (bf16[1,64,2048]{2,1,0:T(8,128)(2,1)S(1)}, bf16[1,64,2048]{2,1,0:T(8,128)(2,1)}, u32[]{:S(2)}) copy-start(bf16[1,64,2048]{2,1,0:T(8,128)(2,1)} %copy.133) | copy-start | bytes 786436
  104.0 9.7 %copy-start.2 = (bf16[64,2,32,32]{0,3,2,1:T(8,128)(2,1)S(1)}, bf16[64,2,32,32]{0,3,2,1:T(8,128)(2,1)}, u32[]{:S(2)}) copy-start(bf16[64,2,32,32]{0,3,2,1:T(8,128)(2,1)} %get-tuple-element.40) | copy-start | bytes 786436
  105.2 14.2 %all-to-all-start.1 = ((bf16[16,2,1024]{2,1,0:T(2,128)(2,1)}), bf16[16,2,1024]{2,1,0:T(2,128)(2,1)}, u32[]{:S(2)}, u32[]{:S(2)}) async-start(bf16[16,2,1024]{2,1,0:T(2,128)(2,1)} %reshape.403), calls=%async_computation.1 | async-start | bytes 131072 | tf_op jit(solution)/shard_map/all_to_all | solution.py:74
  110.3 11.3 %copy-start = (bf16[256,1024]{1,0:T(8,128)(2,1)S(1)}, bf16[256,1024]{1,0:T(8,128)(2,1)}, u32[]{:S(2)}) copy-start(bf16[256,1024]{1,0:T(8,128)(2,1)} %convert_element_type.178) | copy-start | bytes 1572868
  113.6 8.5 %copy-start.18 = (f32[8,8,2,1024]{3,1,2,0:T(8,128)S(1)}, f32[8,8,2,1024]{3,1,2,0:T(8,128)}, u32[]{:S(2)}) copy-start(f32[8,8,2,1024]{3,1,2,0:T(8,128)} %copy.190) | copy-start | bytes 1572868
  122.1 4.7 copy-start.56
  122.1 4.7 copy-start.58
  122.1 4.7 copy-start.60
  124.7 33.7 %copy-start.13 = (bf16[64,2048]{1,0:T(8,128)(2,1)}, bf16[64,2048]{1,0:T(8,128)(2,1)S(1)}, u32[]{:S(2)}) copy-start(bf16[64,2048]{1,0:T(8,128)(2,1)S(1)} %get-tuple-element.68) | copy-start | bytes 786436
  124.7 3.2 copy-start.52
  124.7 3.2 copy-start.54
  134.1 7.0 %copy-start.88 = (f32[3,1,64,64]{3,2,0,1:T(8,128)S(1)}, f32[3,1,64,64]{3,2,0,1:T(8,128)}, u32[]{:S(2)}) copy-start(f32[3,1,64,64]{3,2,0,1:T(8,128)} %convolution_bitcast_fusion.20) | copy-start | bytes 147460
  134.1 7.0 %copy-start.89 = (f32[3,1,64,64]{3,2,0,1:T(8,128)S(1)}, f32[3,1,64,64]{3,2,0,1:T(8,128)}, u32[]{:S(2)}) copy-start(f32[3,1,64,64]{3,2,0,1:T(8,128)} %convolution_bitcast_fusion.19) | copy-start | bytes 147460
  134.1 7.1 %copy-start.83 = (f32[3,1,64,64]{3,2,0,1:T(8,128)S(1)}, f32[3,1,64,64]{3,2,0,1:T(8,128)}, u32[]{:S(2)}) copy-start(f32[3,1,64,64]{3,2,0,1:T(8,128)} %convolution_bitcast_fusion.25) | copy-start | bytes 147460
  134.1 7.1 %copy-start.84 = (f32[3,1,64,64]{3,2,0,1:T(8,128)S(1)}, f32[3,1,64,64]{3,2,0,1:T(8,128)}, u32[]{:S(2)}) copy-start(f32[3,1,64,64]{3,2,0,1:T(8,128)} %convolution_bitcast_fusion.24) | copy-start | bytes 147460
  134.1 7.1 %copy-start.85 = (f32[3,1,64,64]{3,2,0,1:T(8,128)S(1)}, f32[3,1,64,64]{3,2,0,1:T(8,128)}, u32[]{:S(2)}) copy-start(f32[3,1,64,64]{3,2,0,1:T(8,128)} %convolution_bitcast_fusion.23) | copy-start | bytes 147460
  134.1 7.1 %copy-start.86 = (f32[3,1,64,64]{3,2,0,1:T(8,128)S(1)}, f32[3,1,64,64]{3,2,0,1:T(8,128)}, u32[]{:S(2)}) copy-start(f32[3,1,64,64]{3,2,0,1:T(8,128)} %convolution_bitcast_fusion.22) | copy-start | bytes 147460
  134.1 7.1 %copy-start.87 = (f32[3,1,64,64]{3,2,0,1:T(8,128)S(1)}, f32[3,1,64,64]{3,2,0,1:T(8,128)}, u32[]{:S(2)}) copy-start(f32[3,1,64,64]{3,2,0,1:T(8,128)} %convolution_bitcast_fusion.21) | copy-start | bytes 147460
  134.5 6.6 %copy-start.90 = (f32[3,1,64,64]{3,2,0,1:T(8,128)S(1)}, f32[3,1,64,64]{3,2,0,1:T(8,128)}, u32[]{:S(2)}) copy-start(f32[3,1,64,64]{3,2,0,1:T(8,128)} %convolution_bitcast_fusion.18) | copy-start | bytes 147460
  136.7 13.4 %all-to-all-start.2 = ((bf16[16,2,1024]{2,1,0:T(2,128)(2,1)}), bf16[16,2,1024]{2,1,0:T(2,128)(2,1)S(1)}, u32[]{:S(2)}, u32[]{:S(2)}) async-start(bf16[16,2,1024]{2,1,0:T(2,128)(2,1)} %reshape.405), calls=%async_computation.2 | async-start | bytes 131072 | tf_op jit(solution)/shard_map/all_to_all | solution.py:70
  141.1 263.8 %all-reduce.4.cloned.1.call-start = ((), (), s32[]{:S(2)}) async-start(), calls=%async_computation.7 | async-start | bytes 1769472 | tf_op jit(solution)/shard_map/psum | solution.py:194
  142.3 362.8 %reduce-scatter.2.cloned.1.call-start = ((), (), s32[]{:S(2)}) async-start(), calls=%async_computation.6 | async-start | bytes 6684672 | tf_op jit(solution)/shard_map/reduce_scatter | solution.py:169
  159.6 17.6 %collective-permute-start.2 = (bf16[64,1,1024]{0,2,1:T(8,128)(2,1)S(1)}, bf16[64,1,1024]{0,2,1:T(8,128)(2,1)S(1)}, u32[]{:S(2)}, u32[]{:S(2)}) collective-permute-start(bf16[64,1,1024]{0,2,1:T(8,128)(2,1)S(1)} %get-tuple-element.66), channel_id=1, source_target_pairs={{0,1},{1,2},{2,3},{3,4},{4,5},{5,6},{6,7},{7,8},{8,9},{9,10},{10,1... | collective-permute-start | bytes 393224 | tf_op jit(solution)/shard_map/ppermute | solution.py:24
  162.2 15.0 %collective-permute-start.3 = (bf16[64,1,1024]{0,2,1:T(8,128)(2,1)S(1)}, bf16[64,1,1024]{0,2,1:T(8,128)(2,1)S(1)}, u32[]{:S(2)}, u32[]{:S(2)}) collective-permute-start(bf16[64,1,1024]{0,2,1:T(8,128)(2,1)S(1)} %get-tuple-element.67), channel_id=1, source_target_pairs={{1,0},{2,1},{3,2},{4,3},{5,4},{6,5},{7,6},{8,7},{9,8},{10,9},{11,1... | collective-permute-start | bytes 393224 | tf_op jit(solution)/shard_map/ppermute | solution.py:26
  170.8 236.3 %all-to-all-start.3 = ((bf16[16,2,1024]{2,1,0:T(2,128)(2,1)}), bf16[16,2,1024]{2,1,0:T(2,128)(2,1)S(1)}, u32[]{:S(2)}, u32[]{:S(2)}) async-start(bf16[16,2,1024]{2,1,0:T(2,128)(2,1)} %reshape.407), calls=%async_computation.3 | async-start | bytes 131072 | tf_op jit(solution)/shard_map/all_to_all | solution.py:74
  192.8 13.0 %copy-start.10 = (bf16[64,2,32,32]{0,3,2,1:T(8,128)(2,1)S(1)}, bf16[64,2,32,32]{0,3,2,1:T(8,128)(2,1)}, u32[]{:S(2)}) copy-start(bf16[64,2,32,32]{0,3,2,1:T(8,128)(2,1)} %get-tuple-element.23) | copy-start | bytes 786436
  194.1 12.6 %copy-start.8 = (bf16[64,2,32,32]{0,3,2,1:T(8,128)(2,1)S(1)}, bf16[64,2,32,32]{0,3,2,1:T(8,128)(2,1)}, u32[]{:S(2)}) copy-start(bf16[64,2,32,32]{0,3,2,1:T(8,128)(2,1)} %get-tuple-element.24) | copy-start | bytes 786436
  206.7 11.6 %copy-start.6 = (bf16[64,2,32,32]{0,3,2,1:T(8,128)(2,1)S(1)}, bf16[64,2,32,32]{0,3,2,1:T(8,128)(2,1)}, u32[]{:S(2)}) copy-start(bf16[64,2,32,32]{0,3,2,1:T(8,128)(2,1)} %get-tuple-element.31) | copy-start | bytes 786436
  207.6 11.6 %copy-start.4 = (bf16[64,2,32,32]{0,3,2,1:T(8,128)(2,1)S(1)}, bf16[64,2,32,32]{0,3,2,1:T(8,128)(2,1)}, u32[]{:S(2)}) copy-start(bf16[64,2,32,32]{0,3,2,1:T(8,128)(2,1)} %get-tuple-element.32) | copy-start | bytes 786436
  218.3 3.6 copy-start.14
  219.2 4.2 copy-start.17
  220.1 3.3 copy-start.61
  221.9 4.9 copy-start.67
  221.9 4.9 copy-start.68
  221.9 4.9 copy-start.69
  223.4 4.6 copy-start.70
  223.4 4.6 copy-start.71
  223.4 4.6 copy-start.72
  224.6 4.6 copy-start.73
  224.6 4.6 copy-start.74
  224.6 4.6 copy-start.75
  226.9 3.4 copy-start.76
  226.9 3.4 copy-start.77
  226.9 3.4 copy-start.79
  228.0 3.4 copy-start.43
  228.0 3.4 copy-start.46
  228.0 3.4 copy-start.78
  (38 other events, 75.5 us)
Sparse Core Ops, SparseCore 0:
  10.7 71.3 all-gather.1
  148.0 256.8 all-reduce.3
  409.9 95.1 reduce-scatter.1
where the time goes:
time: 520 us; the launch traced here: 514 us
  waiting for transfers between devices  281 us (54%)
  local copies, waits for them, and re-layouts  117 us (22%)
  matrix products  47.2 us (9%)
  starting transfers between devices  36.8 us (7%)
  other arithmetic  17.1 us (3%)
  between operations  15.2 us (3%)
    psum x1, waiting for transfers between devices, shards(): kernel_total = lax.psum(kernel_local, ('batch', 'space'))  172 us
    reduce_scatter x1, waiting for transfers between devices, shards(): lax.psum_scatter(jnp.einsum('ipxy,opxy->xypio', coef, mixed_grad, preferr...  92.8 us
    another operation x53, local copies, waits for them, and re-layouts, stacked_window(): jnp.stack([window[:, offset_z:offset_z + depth_cells] for offset_z in ran...  76.6 us
    dot_general x18, matrix products, stencil(): lax.dot_general(kernel[:, offset_x, offset_y], stacked, (((0, 1), (0, 1))...  22.9 us
    all_to_all x2, starting transfers between devices, to_pencils(): lax.all_to_all(values, 'space', split_axis=3, concat_axis=1, tiled=True)  15.8 us
    all_to_all x2, starting transfers between devices, to_slabs(): lax.all_to_all(values, 'space', split_axis=1, concat_axis=3, tiled=True)  11.5 us
    all_to_all x2, waiting for transfers between devices, to_pencils(): lax.all_to_all(values, 'space', split_axis=3, concat_axis=1, tiled=True)  11.2 us
    slice x4, local copies, waits for them, and re-layouts, stacked_window(): window[:, offset_z:offset_z + depth_cells]  10.7 us
  transfers between devices with their start and end apart: 11, of which 5 were waited for; matrix products, arithmetic and copies ran while one was open for 30% of the time, Pallas kernels for 0%

commit v1 on v0

--- a/solution.py
+++ b/solution.py
@@ -191,7 +191,7 @@
         .reshape(channels, depth_cells, plane)
     )
     kernel_local = kernel_terms(padded, pre_grad)
-    kernel_total = lax.psum(kernel_local, ("batch", "space"))
+    kernel_total = lax.psum(lax.psum(kernel_local, "batch"), "space")
     conv_gradient = kernel_total / math.sqrt(lax.axis_size("batch") * total_depth * plane)
     return (activated[None], input_gradient[None], mode_gradient, conv_gradient)
 

time: 520 us -> 553 us (1.063)
  waiting for transfers between devices: 281 us -> 310 us
    psum x1 -> x2, waiting for transfers between devices: 172 us -> 195 us  [shards(): kernel_total = lax.psum(lax.psum(kernel_local, 'batch'), 'space')]
    reduce_scatter x1, waiting for transfers between devices: 92.8 us -> 99.1 us  [shards(): lax.psum_scatter(jnp.einsum('ipxy,opxy->xypio', coef, mixed_grad, preferr...]
  transfers between devices with their start and end apart: 11 -> 12, of which waited for: 5 -> 6; matrix products, arithmetic and copies ran while one was open for 30% -> 28% of each run, Pallas kernels for 0% -> 0%
where the time goes in v1:
time: 553 us; the launch traced here: 547 us
  waiting for transfers between devices  310 us (56%)
  local copies, waits for them, and re-layouts  116 us (21%)
  matrix products  47.2 us (9%)
  starting transfers between devices  41.7 us (8%)
  other arithmetic  17.1 us (3%)
  between operations  15.2 us (3%)
    psum x2, waiting for transfers between devices, shards(): kernel_total = lax.psum(lax.psum(kernel_local, 'batch'), 'space')  195 us
    reduce_scatter x1, waiting for transfers between devices, shards(): lax.psum_scatter(jnp.einsum('ipxy,opxy->xypio', coef, mixed_grad, preferr...  99.1 us
    another operation x53, local copies, waits for them, and re-layouts, stacked_window(): jnp.stack([window[:, offset_z:offset_z + depth_cells] for offset_z in ran...  76.4 us
    dot_general x18, matrix products, stencil(): lax.dot_general(kernel[:, offset_x, offset_y], stacked, (((0, 1), (0, 1))...  22.9 us
    all_to_all x2, starting transfers between devices, to_pencils(): lax.all_to_all(values, 'space', split_axis=3, concat_axis=1, tiled=True)  15.8 us
    all_to_all x2, starting transfers between devices, to_slabs(): lax.all_to_all(values, 'space', split_axis=1, concat_axis=3, tiled=True)  15.8 us
    all_to_all x2, waiting for transfers between devices, to_pencils(): lax.all_to_all(values, 'space', split_axis=3, concat_axis=1, tiled=True)  11.2 us
  transfers between devices with their start and end apart: 12, of which 6 were waited for; matrix products, arithmetic and copies ran while one was open for 28% of the time, Pallas kernels for 0%

profile of v1, /device:TPU:2, one launch (start us, length us, event | category | flops | bytes accessed | tf_op | source)
XLA Modules:
  0.0 547.0 jit_solution(1824815242478243762)
XLA Ops:
  10.0 4.2 collective-permute-start
  15.5 1.8 reshape_squeeze.4
  17.3 2.2 fusion.6
  19.5 3.6 convert_element_type.165
  25.6 1.8 copy.99
  28.2 11.5 %all-to-all-start = ((bf16[16,2,1024]{2,1,0:T(2,128)(2,1)}), bf16[16,2,1024]{2,1,0:T(2,128)(2,1)S(1)}, u32[]{:S(2)}, u32[]{:S(2)}) async-start(bf16[16,2,1024]{2,1,0:T(2,128)(2,1)} %reshape.401), calls=%async_computation | async-start | bytes 131072 | tf_op jit(solution)/shard_map/all_to_all | solution.py:70
  40.6 1.8 copy.190
  42.4 2.9 convert_element_type.178
  45.3 3.4 all-to-all-done
  53.0 1.6 select_maximum_fusion.2
  54.5 1.5 fusion.196
  56.0 1.9 copy.109
  58.0 1.9 copy.107
  61.7 3.9 fusion.195
  65.6 2.0 copy.134
  67.6 2.0 copy.133
  69.6 1.9 copy.132
  71.5 1.9 copy.130
  73.5 1.9 copy.129
  75.4 1.9 copy.128
  77.4 1.9 copy.126
  81.1 2.0 copy.119
  83.1 2.0 copy.118
  85.1 1.9 copy.117
  87.0 1.9 copy.115
  88.9 1.9 copy.114
  93.6 1.4 convolution_bitcast_fusion.17
  95.1 1.5 fusion.19
  99.3 4.6 fusion.3
  105.0 5.2 all-to-all-start.1
  110.3 2.4 fusion.13
  115.4 3.9 all-to-all-done.1
  122.0 2.6 fusion.85
  124.6 2.1 convolution_bitcast_fusion.25
  136.7 4.3 all-to-all-start.2
  142.3 7.8 %all-to-all-done.2 = bf16[16,2,1024]{2,1,0:T(2,128)(2,1)S(1)} async-done(((bf16[16,2,1024]{2,1,0:T(2,128)(2,1)}), bf16[16,2,1024]{2,1,0:T(2,128)(2,1)S(1)}, u32[]{:S(2)}, u32[]{:S(2)}) %all-to-all-start.2) | async-done | bytes 65568 | tf_op jit(solution)/shard_map/all_to_all | solution.py:70
  150.6 134.2 %all-reduce.5.cloned.1.call-done = f32[3,3,3,64,64]{4,3,0,2,1:T(8,128)} async-done(((f32[3,3,3,64,64]{4,3,0,2,1:T(8,128)}), f32[3,3,3,64,64]{4,3,0,2,1:T(8,128)}) %all-reduce.5.cloned.1.call-update) | async-done | bytes 442384 | tf_op jit(solution)/shard_map/psum | solution.py:194
  284.9 5.8 %fusion = bf16[16,1,24,64,64]{4,3,2,1,0:T(8,128)(2,1)} fusion(f32[16,24,64]{2,1,0:T(8,128)S(1)} %get-tuple-element.76, f32[16,24,64]{2,1,0:T(8,128)S(1)} %get-tuple-element.77), kind=kLoop, calls=%fused_computation.1 | loop fusion | flops 3145728 | bytes 3342336 | tf_op jit(solution)/shard_map/convert_element_type | solution.py:170
  293.8 3.1 collective-permute-start.2
  296.9 1.3 collective-permute-start.3
  298.2 6.1 %fusion.1 = bf16[24,16,1,64]{3,2,1,0:T(2,128)(2,1)S(1)} fusion(bf16[64,24,16,1]{0,1,2,3:T(8,128)(2,1)S(1)} %bitcast.459, bf16[16,1,24,64,64]{4,3,2,1,0:T(8,128)(2,1)} %all-gather.2.cloned.1.call-done), kind=kOutput, calls=%fused_computation.4 | convolution fusion | flops 3145728 | bytes 3244032 | tf_op jit(solution)/shard_map/opxy,xypio->ipxy/dot_general | solution.py:166
  305.5 10.6 %all-to-all-start.3 = ((bf16[16,2,1024]{2,1,0:T(2,128)(2,1)}), bf16[16,2,1024]{2,1,0:T(2,128)(2,1)S(1)}, u32[]{:S(2)}, u32[]{:S(2)}) async-start(bf16[16,2,1024]{2,1,0:T(2,128)(2,1)} %reshape.407), calls=%async_computation.3 | async-start | bytes 131072 | tf_op jit(solution)/shard_map/all_to_all | solution.py:74
  318.2 1.6 select_maximum_fusion
  319.8 1.4 fusion.194
  321.3 1.9 copy.148
  323.2 1.9 copy.152
  327.8 3.8 fusion.193
  333.0 2.0 copy.172
  335.0 1.9 copy.171
  336.9 1.9 copy.170
  338.8 1.9 copy.169
  340.8 1.9 copy.168
  342.7 1.9 copy.167
  346.4 2.0 copy.164
  348.5 1.9 copy.163
  350.4 1.9 copy.162
  352.3 1.9 copy.159
  354.3 1.9 copy.158
  360.8 1.4 convolution_bitcast_fusion.4
  363.4 2.3 convolution_bitcast_fusion.1
  373.2 2.4 fusion.30
  376.5 60.5 %all-reduce.7.cloned.1.call-done = f32[3,3,3,64,64]{4,3,0,2,1:T(8,128)} async-done(((f32[3,3,3,64,64]{4,3,0,2,1:T(8,128)}), f32[3,3,3,64,64]{4,3,0,2,1:T(8,128)}) %all-reduce.7.cloned.1.call-update) | async-done | bytes 442384 | tf_op jit(solution)/shard_map/psum | solution.py:194
  439.2 99.1 %reduce-scatter.2.cloned.1.call-done = bf16[1,1,24,64,64]{4,3,2,1,0:T(8,128)(2,1)} async-done(((bf16[16,1,24,64,64]{4,3,2,1,0:T(8,128)(2,1)}), bf16[1,1,24,64,64]{4,3,2,1,0:T(8,128)(2,1)}) %reduce-scatter.2.cloned.1.call-update) | async-done | bytes 196624 | tf_op jit(solution)/shard_map/reduce_scatter | solution.py:169
  538.3 2.0 convert_element_type.196
  (296 shorter events, 67.9 us)
Async XLA Ops:
  7.2 92.1 %all-gather.2.cloned.1.call-start = ((), (), s32[]{:S(2)}) async-start(), calls=%async_computation.5 | async-start | bytes 6684672 | tf_op jit(solution)/shard_map/all_gather | solution.py:135
  10.0 40.0 %collective-permute-start = (bf16[64,1,1024]{0,2,1:T(8,128)(2,1)}, bf16[64,1,1024]{0,2,1:T(8,128)(2,1)}, u32[]{:S(2)}, u32[]{:S(2)}) collective-permute-start(bf16[64,1,1024]{0,2,1:T(8,128)(2,1)} %get-tuple-element.72), channel_id=1, source_target_pairs={{0,1},{1,2},{2,3},{3,4},{4,5},{5,6},{6,7},{7,8},{8,9},{9,10},{10,1... | collective-permute-start | bytes 393224 | tf_op jit(solution)/shard_map/ppermute | solution.py:24
  14.2 35.8 %collective-permute-start.1 = (bf16[64,1,1024]{0,2,1:T(8,128)(2,1)}, bf16[64,1,1024]{0,2,1:T(8,128)(2,1)}, u32[]{:S(2)}, u32[]{:S(2)}) collective-permute-start(bf16[64,1,1024]{0,2,1:T(8,128)(2,1)} %get-tuple-element.73), channel_id=1, source_target_pairs={{1,0},{2,1},{3,2},{4,3},{5,4},{6,5},{7,6},{8,7},{9,8},{10,9},{11,1... | collective-permute-start | bytes 393224 | tf_op jit(solution)/shard_map/ppermute | solution.py:26
  19.5 20.2 %copy-start.1 = (bf16[1,64,2,1024]{3,2,1,0:T(2,128)(2,1)S(1)}, bf16[1,64,2,1024]{3,2,1,0:T(2,128)(2,1)}, u32[]{:S(2)}) copy-start(bf16[1,64,2,1024]{3,2,1,0:T(2,128)(2,1)} %param.4) | copy-start | bytes 786436
  28.2 20.6 %all-to-all-start = ((bf16[16,2,1024]{2,1,0:T(2,128)(2,1)}), bf16[16,2,1024]{2,1,0:T(2,128)(2,1)S(1)}, u32[]{:S(2)}, u32[]{:S(2)}) async-start(bf16[16,2,1024]{2,1,0:T(2,128)(2,1)} %reshape.401), calls=%async_computation | async-start | bytes 131072 | tf_op jit(solution)/shard_map/all_to_all | solution.py:70
  65.6 13.7 %copy-start.9 = (bf16[64,2,32,32]{0,3,2,1:T(8,128)(2,1)S(1)}, bf16[64,2,32,32]{0,3,2,1:T(8,128)(2,1)}, u32[]{:S(2)}) copy-start(bf16[64,2,32,32]{0,3,2,1:T(8,128)(2,1)} %get-tuple-element.49) | copy-start | bytes 786436
  67.6 12.6 %copy-start.7 = (bf16[64,2,32,32]{0,3,2,1:T(8,128)(2,1)S(1)}, bf16[64,2,32,32]{0,3,2,1:T(8,128)(2,1)}, u32[]{:S(2)}) copy-start(bf16[64,2,32,32]{0,3,2,1:T(8,128)(2,1)} %get-tuple-element.50) | copy-start | bytes 786436
  80.2 11.6 %copy-start.5 = (bf16[64,2,32,32]{0,3,2,1:T(8,128)(2,1)S(1)}, bf16[64,2,32,32]{0,3,2,1:T(8,128)(2,1)}, u32[]{:S(2)}) copy-start(bf16[64,2,32,32]{0,3,2,1:T(8,128)(2,1)} %get-tuple-element.57) | copy-start | bytes 786436
  81.1 11.6 %copy-start.3 = (bf16[64,2,32,32]{0,3,2,1:T(8,128)(2,1)S(1)}, bf16[64,2,32,32]{0,3,2,1:T(8,128)(2,1)}, u32[]{:S(2)}) copy-start(bf16[64,2,32,32]{0,3,2,1:T(8,128)(2,1)} %get-tuple-element.58) | copy-start | bytes 786436
  83.1 10.5 %copy-start.22 = (bf16[1,64,2048]{2,1,0:T(8,128)(2,1)S(1)}, bf16[1,64,2048]{2,1,0:T(8,128)(2,1)}, u32[]{:S(2)}) copy-start(bf16[1,64,2048]{2,1,0:T(8,128)(2,1)} %copy.107) | copy-start | bytes 786436
  91.8 3.3 copy-start.19
  92.7 3.9 copy-start.55
  92.7 3.9 copy-start.57
  93.6 3.3 copy-start.49
  93.6 3.3 copy-start.51
  93.6 3.4 copy-start.53
  99.3 11.0 %copy-start.30 = (bf16[1,64,2048]{2,1,0:T(8,128)(2,1)S(1)}, bf16[1,64,2048]{2,1,0:T(8,128)(2,1)}, u32[]{:S(2)}) copy-start(bf16[1,64,2048]{2,1,0:T(8,128)(2,1)} %copy.134) | copy-start | bytes 786436
  99.3 11.0 %copy-start.32 = (bf16[1,64,2048]{2,1,0:T(8,128)(2,1)S(1)}, bf16[1,64,2048]{2,1,0:T(8,128)(2,1)}, u32[]{:S(2)}) copy-start(bf16[1,64,2048]{2,1,0:T(8,128)(2,1)} %copy.133) | copy-start | bytes 786436
  103.9 9.7 %copy-start.2 = (bf16[64,2,32,32]{0,3,2,1:T(8,128)(2,1)S(1)}, bf16[64,2,32,32]{0,3,2,1:T(8,128)(2,1)}, u32[]{:S(2)}) copy-start(bf16[64,2,32,32]{0,3,2,1:T(8,128)(2,1)} %get-tuple-element.40) | copy-start | bytes 786436
  105.0 14.3 %all-to-all-start.1 = ((bf16[16,2,1024]{2,1,0:T(2,128)(2,1)}), bf16[16,2,1024]{2,1,0:T(2,128)(2,1)}, u32[]{:S(2)}, u32[]{:S(2)}) async-start(bf16[16,2,1024]{2,1,0:T(2,128)(2,1)} %reshape.403), calls=%async_computation.1 | async-start | bytes 131072 | tf_op jit(solution)/shard_map/all_to_all | solution.py:74
  110.3 11.3 %copy-start = (bf16[256,1024]{1,0:T(8,128)(2,1)S(1)}, bf16[256,1024]{1,0:T(8,128)(2,1)}, u32[]{:S(2)}) copy-start(bf16[256,1024]{1,0:T(8,128)(2,1)} %convert_element_type.178) | copy-start | bytes 1572868
  113.5 8.5 %copy-start.18 = (f32[8,8,2,1024]{3,1,2,0:T(8,128)S(1)}, f32[8,8,2,1024]{3,1,2,0:T(8,128)}, u32[]{:S(2)}) copy-start(f32[8,8,2,1024]{3,1,2,0:T(8,128)} %copy.190) | copy-start | bytes 1572868
  122.0 4.7 copy-start.56
  122.0 4.7 copy-start.58
  122.0 4.7 copy-start.60
  124.6 168.0 %copy-start.13 = (bf16[64,2048]{1,0:T(8,128)(2,1)}, bf16[64,2048]{1,0:T(8,128)(2,1)S(1)}, u32[]{:S(2)}) copy-start(bf16[64,2048]{1,0:T(8,128)(2,1)S(1)} %get-tuple-element.68) | copy-start | bytes 786436
  124.6 3.2 copy-start.54
  134.0 7.0 %copy-start.88 = (f32[3,1,64,64]{3,2,0,1:T(8,128)S(1)}, f32[3,1,64,64]{3,2,0,1:T(8,128)}, u32[]{:S(2)}) copy-start(f32[3,1,64,64]{3,2,0,1:T(8,128)} %convolution_bitcast_fusion.20) | copy-start | bytes 147460
  134.0 7.0 %copy-start.89 = (f32[3,1,64,64]{3,2,0,1:T(8,128)S(1)}, f32[3,1,64,64]{3,2,0,1:T(8,128)}, u32[]{:S(2)}) copy-start(f32[3,1,64,64]{3,2,0,1:T(8,128)} %convolution_bitcast_fusion.19) | copy-start | bytes 147460
  134.0 7.1 %copy-start.83 = (f32[3,1,64,64]{3,2,0,1:T(8,128)S(1)}, f32[3,1,64,64]{3,2,0,1:T(8,128)}, u32[]{:S(2)}) copy-start(f32[3,1,64,64]{3,2,0,1:T(8,128)} %convolution_bitcast_fusion.25) | copy-start | bytes 147460
  134.0 7.1 %copy-start.84 = (f32[3,1,64,64]{3,2,0,1:T(8,128)S(1)}, f32[3,1,64,64]{3,2,0,1:T(8,128)}, u32[]{:S(2)}) copy-start(f32[3,1,64,64]{3,2,0,1:T(8,128)} %convolution_bitcast_fusion.24) | copy-start | bytes 147460
  134.1 7.1 %copy-start.85 = (f32[3,1,64,64]{3,2,0,1:T(8,128)S(1)}, f32[3,1,64,64]{3,2,0,1:T(8,128)}, u32[]{:S(2)}) copy-start(f32[3,1,64,64]{3,2,0,1:T(8,128)} %convolution_bitcast_fusion.23) | copy-start | bytes 147460
  134.1 7.1 %copy-start.86 = (f32[3,1,64,64]{3,2,0,1:T(8,128)S(1)}, f32[3,1,64,64]{3,2,0,1:T(8,128)}, u32[]{:S(2)}) copy-start(f32[3,1,64,64]{3,2,0,1:T(8,128)} %convolution_bitcast_fusion.22) | copy-start | bytes 147460
  134.1 7.1 %copy-start.87 = (f32[3,1,64,64]{3,2,0,1:T(8,128)S(1)}, f32[3,1,64,64]{3,2,0,1:T(8,128)}, u32[]{:S(2)}) copy-start(f32[3,1,64,64]{3,2,0,1:T(8,128)} %convolution_bitcast_fusion.21) | copy-start | bytes 147460
  134.4 6.6 %copy-start.90 = (f32[3,1,64,64]{3,2,0,1:T(8,128)S(1)}, f32[3,1,64,64]{3,2,0,1:T(8,128)}, u32[]{:S(2)}) copy-start(f32[3,1,64,64]{3,2,0,1:T(8,128)} %convolution_bitcast_fusion.18) | copy-start | bytes 147460
  136.7 13.4 %all-to-all-start.2 = ((bf16[16,2,1024]{2,1,0:T(2,128)(2,1)}), bf16[16,2,1024]{2,1,0:T(2,128)(2,1)S(1)}, u32[]{:S(2)}, u32[]{:S(2)}) async-start(bf16[16,2,1024]{2,1,0:T(2,128)(2,1)} %reshape.405), calls=%async_computation.2 | async-start | bytes 131072 | tf_op jit(solution)/shard_map/all_to_all | solution.py:70
  141.0 143.8 %all-reduce.5.cloned.1.call-start = ((), (), s32[]{:S(2)}) async-start(), calls=%async_computation.7 | async-start | bytes 1769472 | tf_op jit(solution)/shard_map/psum | solution.py:194
  142.2 294.7 %all-reduce.7.cloned.1.call-start = ((), (), s32[]{:S(2)}) async-start(), calls=%async_computation.8 | async-start | bytes 1769472 | tf_op jit(solution)/shard_map/psum | solution.py:194
  284.8 253.5 %reduce-scatter.2.cloned.1.call-start = ((), (), s32[]{:S(2)}) async-start(), calls=%async_computation.6 | async-start | bytes 6684672 | tf_op jit(solution)/shard_map/reduce_scatter | solution.py:169
  293.8 22.4 %collective-permute-start.2 = (bf16[64,1,1024]{0,2,1:T(8,128)(2,1)S(1)}, bf16[64,1,1024]{0,2,1:T(8,128)(2,1)S(1)}, u32[]{:S(2)}, u32[]{:S(2)}) collective-permute-start(bf16[64,1,1024]{0,2,1:T(8,128)(2,1)S(1)} %get-tuple-element.66), channel_id=1, source_target_pairs={{0,1},{1,2},{2,3},{3,4},{4,5},{5,6},{6,7},{7,8},{8,9},{9,10},{10,1... | collective-permute-start | bytes 393224 | tf_op jit(solution)/shard_map/ppermute | solution.py:24
  296.9 19.3 %collective-permute-start.3 = (bf16[64,1,1024]{0,2,1:T(8,128)(2,1)S(1)}, bf16[64,1,1024]{0,2,1:T(8,128)(2,1)S(1)}, u32[]{:S(2)}, u32[]{:S(2)}) collective-permute-start(bf16[64,1,1024]{0,2,1:T(8,128)(2,1)S(1)} %get-tuple-element.67), channel_id=1, source_target_pairs={{1,0},{2,1},{3,2},{4,3},{5,4},{6,5},{7,6},{8,7},{9,8},{10,9},{11,1... | collective-permute-start | bytes 393224 | tf_op jit(solution)/shard_map/ppermute | solution.py:26
  305.5 65.8 %all-to-all-start.3 = ((bf16[16,2,1024]{2,1,0:T(2,128)(2,1)}), bf16[16,2,1024]{2,1,0:T(2,128)(2,1)S(1)}, u32[]{:S(2)}, u32[]{:S(2)}) async-start(bf16[16,2,1024]{2,1,0:T(2,128)(2,1)} %reshape.407), calls=%async_computation.3 | async-start | bytes 131072 | tf_op jit(solution)/shard_map/all_to_all | solution.py:74
  331.6 13.0 %copy-start.10 = (bf16[64,2,32,32]{0,3,2,1:T(8,128)(2,1)S(1)}, bf16[64,2,32,32]{0,3,2,1:T(8,128)(2,1)}, u32[]{:S(2)}) copy-start(bf16[64,2,32,32]{0,3,2,1:T(8,128)(2,1)} %get-tuple-element.23) | copy-start | bytes 786436
  333.0 12.6 %copy-start.8 = (bf16[64,2,32,32]{0,3,2,1:T(8,128)(2,1)S(1)}, bf16[64,2,32,32]{0,3,2,1:T(8,128)(2,1)}, u32[]{:S(2)}) copy-start(bf16[64,2,32,32]{0,3,2,1:T(8,128)(2,1)} %get-tuple-element.24) | copy-start | bytes 786436
  345.5 11.6 %copy-start.6 = (bf16[64,2,32,32]{0,3,2,1:T(8,128)(2,1)S(1)}, bf16[64,2,32,32]{0,3,2,1:T(8,128)(2,1)}, u32[]{:S(2)}) copy-start(bf16[64,2,32,32]{0,3,2,1:T(8,128)(2,1)} %get-tuple-element.31) | copy-start | bytes 786436
  346.4 11.6 %copy-start.4 = (bf16[64,2,32,32]{0,3,2,1:T(8,128)(2,1)S(1)}, bf16[64,2,32,32]{0,3,2,1:T(8,128)(2,1)}, u32[]{:S(2)}) copy-start(bf16[64,2,32,32]{0,3,2,1:T(8,128)(2,1)} %get-tuple-element.32) | copy-start | bytes 786436
  357.1 3.7 copy-start.14
  358.0 4.2 copy-start.17
  358.9 3.3 copy-start.61
  360.8 4.9 copy-start.67
  360.8 4.9 copy-start.68
  360.8 4.9 copy-start.69
  362.2 4.6 copy-start.70
  362.3 4.6 copy-start.71
  362.3 4.6 copy-start.72
  363.4 4.6 copy-start.73
  363.4 4.6 copy-start.74
  363.4 4.6 copy-start.75
  365.7 3.4 copy-start.76
  365.7 3.4 copy-start.77
  365.7 3.4 copy-start.79
  366.8 3.4 copy-start.43
  366.8 3.3 copy-start.46
  366.8 3.3 copy-start.78
  (39 other events, 78.8 us)
Sparse Core Ops, SparseCore 0:
  10.7 71.3 all-gather.1
  145.1 139.6 all-reduce.4
  287.6 149.2 all-reduce.6
  441.2 97.0 reduce-scatter.1
